TPU v7x, 256 devices: a whole 4x4x8 slice. The times are simulated.
256 devices in a mesh: seq: 64 (over x_lo, y, z), sub: 4 (over x_hi, core).
Axes of the slice: x: 4 (x_hi: 2, x_lo: 2; x = x_hi * 2 + x_lo), y: 4, z: 8, core: 2. Of those that a mesh axis runs over, the one named last changes fastest.
Arguments:
- normed: bfloat16 [32768, 2048], P(('seq', 'sub')), as said below
- w_query: bfloat16 [2048, 2048], P(None, 'sub'), as said below
- w_key: bfloat16 [2048, 2048], P(None, 'sub'), as said below
- w_value: bfloat16 [2048, 2048], P(None, 'sub'), may hold values from -0.125 to 0.125
- w_out: bfloat16 [2048, 2048], P('sub'), may hold values from -0.25 to 0.25
- pattern: int32 [16, 128], P('sub'), may hold values from 0 to 127, each once within a row
- slide_lengths: int32 [8], replicated, may hold values from 1 to 160, 256 in all
Outputs:
- mixed: bfloat16 [32768, 2048], P(('seq', 'sub'))
Inputs may be any that keep to these rules, and one draw needn't show every extreme that they name: `pattern`: each row is an ordering of the 128 positions of a block. `slide_lengths`: the slides lie end to end and fill all 256 blocks. `normed`: entries of order one. `w_query`: entries of order 2048 ** -0.5. `w_key`: entries of order 2048 ** -0.5.
All inputs are finite; a program needn't handle non-finite values.
Results may differ from a plain program's by a relative error of at most 0.012.
Values may be sent and summed in bfloat16 or wider, within the bound.
A program may use at most 128 MiB of HBM per device.

v0:
```python
import math

import jax
import jax.numpy as jnp
from jax import lax
from jax.sharding import PartitionSpec as P

HEAD_SIZE = 128
BLOCK = 128
DILATED_KEPT = 16


def slide_count(block_index, slide_ends):
    return jnp.sum((block_index[:, None] >= slide_ends[None, :]).astype(jnp.int32), axis=1)


def shards(normed, w_query, w_key, w_value, w_out, pattern, slide_lengths):
    head_cols = w_query.shape[1]
    nearby_heads = head_cols // HEAD_SIZE
    piece = lax.all_gather(normed, "sub", axis=0, tiled=True)
    outputs = [
        jnp.dot(piece, weight, preferred_element_type=jnp.float32).astype(jnp.bfloat16)
        for weight in (w_query, w_key, w_value)
    ]
    projected = jnp.concatenate(outputs, axis=1)
    queries = projected[:, :head_cols]
    keys_all = projected[:, head_cols : 2 * head_cols]
    values_all = projected[:, 2 * head_cols :]
    span_len = projected.shape[0]
    span_of_blocks = span_len // BLOCK
    my_span = lax.axis_index("seq")
    slide_ends = jnp.cumsum(slide_lengths)
    kept_positions = pattern[:, :DILATED_KEPT]

    def dilate(source):
        blocked = source.reshape(span_of_blocks, BLOCK, nearby_heads, HEAD_SIZE)
        selected_keys = [
            blocked[:, kept_positions[head_index], head_index, :]
            for head_index in range(nearby_heads)
        ]
        return jnp.stack(selected_keys).reshape(
            nearby_heads, span_of_blocks * DILATED_KEPT, HEAD_SIZE
        )

    far_keys, far_values = (
        lax.all_gather(dilate(keys_all), "seq", axis=1, tiled=True),
        lax.all_gather(dilate(values_all), "seq", axis=1, tiled=True),
    )
    distant_count = far_keys.shape[1]
    distant_block = jnp.arange(distant_count, dtype=jnp.int32) // DILATED_KEPT
    distant_slide = slide_count(distant_block, slide_ends)
    far_span = distant_block // span_of_blocks
    row_block = my_span * span_of_blocks + jnp.arange(span_len, dtype=jnp.int32) // BLOCK
    row_slide = slide_count(row_block, slide_ends)
    near_mask = row_slide[:, None] == row_slide[None, :]
    far_mask = (row_slide[:, None] == distant_slide[None, :]) & (far_span != my_span)[None, :]
    scale = 1.0 / math.sqrt(HEAD_SIZE)
    outputs = []
    for head_index in range(nearby_heads):
        columns = slice(head_index * HEAD_SIZE, (head_index + 1) * HEAD_SIZE)
        query_head = queries[:, columns]
        near = (
            jnp.einsum(
                "qd,kd->qk", query_head, keys_all[:, columns], preferred_element_type=jnp.float32
            )
            * scale
        )
        far = (
            jnp.einsum(
                "qd,kd->qk", query_head, far_keys[head_index], preferred_element_type=jnp.float32
            )
            * scale
        )
        near = jnp.where(near_mask, near, -1e30)
        far = jnp.where(far_mask, far, -1e30)
        peak = jnp.maximum(
            jnp.max(near, axis=1, keepdims=True), jnp.max(far, axis=1, keepdims=True)
        )
        near_exp = jnp.exp(near - peak)
        far_exp = jnp.exp(far - peak)
        total = jnp.sum(near_exp, axis=1, keepdims=True) + jnp.sum(far_exp, axis=1, keepdims=True)
        near_weight = (near_exp / total).astype(jnp.bfloat16)
        far_weight = (far_exp / total).astype(jnp.bfloat16)
        context_head = jnp.dot(
            near_weight, values_all[:, columns], preferred_element_type=jnp.float32
        )
        context_head = context_head + jnp.dot(
            far_weight, far_values[head_index], preferred_element_type=jnp.float32
        )
        outputs.append(context_head.astype(jnp.bfloat16))
    context = jnp.concatenate(outputs, axis=1)
    return lax.psum_scatter(
        jnp.dot(context, w_out, preferred_element_type=jnp.float32),
        "sub",
        scatter_dimension=0,
        tiled=True,
    ).astype(jnp.bfloat16)


def solution(mesh):
    placed = (
        P(("seq", "sub"), None),
        P(None, "sub"),
        P(None, "sub"),
        P(None, "sub"),
        P("sub", None),
        P("sub", None),
        P(),
    )
    return jax.shard_map(
        shards, mesh=mesh, in_specs=placed, out_specs=P(("seq", "sub"), None), check_vma=False
    )
```

profile of v0, /device:TPU:1, one launch (start us, length us, event | category | flops | bytes accessed | tf_op | source)
XLA Modules:
  0.0 747.2 jit_solution(3258712888125607824)
XLA Ops:
  6.5 0.7 all-gather.4.cloned.1.call-update
  7.3 0.8 fusion.52
  8.2 34.3 %all-gather.4.cloned.1.call-done = bf16[512,2048]{1,0:T(8,128)(2,1)} async-done(((bf16[128,2048]{1,0:T(8,128)(2,1)}), bf16[512,2048]{1,0:T(8,128)(2,1)}) %all-gather.4.cloned.1.call-update) | async-done | bytes 2097168 | tf_op jit(solution)/shard_map/all_gather | solution.py:20
  42.5 3.5 convolution_convert_fusion.1
  46.0 0.8 copy-done.8
  46.9 0.7 copy.32
  47.6 0.6 gather_fusion.2
  48.2 0.6 gather_fusion.3
  48.8 0.6 gather_fusion
  49.5 0.6 gather_fusion.1
  50.1 0.6 pad_maximum_fusion
  50.8 3.5 convolution_convert_fusion
  54.3 0.8 copy-done.6
  55.2 0.7 copy.40
  55.9 0.6 gather_fusion.4
  56.5 0.6 gather_fusion.5
  57.1 0.6 gather_fusion.6
  57.7 0.6 gather_fusion.7
  58.4 0.6 pad_maximum_fusion.1
  59.5 3.5 convolution_convert_fusion.2
  63.0 2.4 fusion.72
  65.4 1.3 fusion.70
  66.7 1.3 fusion.68
  68.0 1.2 fusion.66
  69.3 238.3 %all-gather.6.cloned.1.call-done = bf16[4,4096,128]{2,1,0:T(8,128)(2,1)} async-done(((bf16[4,64,128]{2,1,0:T(8,128)(2,1)}), bf16[4,4096,128]{2,1,0:T(8,128)(2,1)}) %all-gather.6.cloned.1.call-update) | async-done | bytes 4194320 | tf_op jit(solution)/shard_map/all_gather | solution.py:46
  307.6 3.7 fusion.73
  311.4 0.2 fusion.12
  311.6 3.0 copy-done.1
  314.6 1.3 fusion
  315.9 293.8 %all-gather.8.cloned.1.call-done = bf16[4,4096,128]{2,1,0:T(8,128)(2,1)} async-done(((bf16[4,64,128]{2,1,0:T(8,128)(2,1)}), bf16[4,4096,128]{2,1,0:T(8,128)(2,1)}) %all-gather.8.cloned.1.call-update) | async-done | bytes 4194320 | tf_op jit(solution)/shard_map/all_gather | solution.py:47
  609.7 5.2 fusion.4
  614.9 0.3 fusion.8
  615.3 2.4 fusion.71
  617.7 1.3 fusion.1
  619.2 1.0 copy-done.11
  620.2 2.1 fusion.5
  622.3 0.3 fusion.9
  622.6 2.4 fusion.69
  625.0 1.3 fusion.2
  626.5 2.1 fusion.6
  628.6 0.3 fusion.10
  628.9 2.6 fusion.67
  631.6 1.3 fusion.3
  633.0 2.1 fusion.7
  635.1 0.3 fusion.11
  635.5 3.2 fusion.16
  638.7 99.9 %reduce-scatter.2.cloned.1.call-done = f32[128,2048]{1,0:T(8,128)} async-done(((f32[512,2048]{1,0:T(8,128)}), f32[128,2048]{1,0:T(8,128)}) %reduce-scatter.2.cloned.1.call-update) | async-done | bytes 1048592 | tf_op jit(solution)/shard_map/reduce_scatter | solution.py:92
  738.6 2.1 convert_element_type.71
  (60 shorter events, 1.6 us)
Async XLA Ops:
  6.5 628.9 %copy-start = (bf16[512,2048]{1,0:T(8,128)(2,1)S(1)}, bf16[512,2048]{1,0:T(8,128)(2,1)}, u32[]{:S(2)}) copy-start(bf16[512,2048]{1,0:T(8,128)(2,1)} %param.11) | copy-start | bytes 6291460
  6.5 36.0 %all-gather.4.cloned.1.call-start = ((), (), s32[]{:S(2)}) async-start(), calls=%async_computation.1 | async-start | bytes 2621440 | tf_op jit(solution)/shard_map/all_gather | solution.py:20
  7.3 300.3 %all-gather.6.cloned.1.call-start = ((), (), s32[]{:S(2)}) async-start(), calls=%async_computation.2 | async-start | bytes 4259840 | tf_op jit(solution)/shard_map/all_gather | solution.py:46
  8.1 50.9 %copy-start.12 = (s32[8]{0:T(128)S(1)}, s32[8]{0:T(128)}, u32[]{:S(2)}) copy-start(s32[8]{0:T(128)} %param.13) | copy-start | bytes 100
  46.0 0.8 copy-start.8
  50.7 558.9 %all-gather.8.cloned.1.call-start = ((), (), s32[]{:S(2)}) async-start(), calls=%async_computation.3 | async-start | bytes 4259840 | tf_op jit(solution)/shard_map/all_gather | solution.py:47
  54.3 0.8 copy-start.6
  55.9 9.5 %copy-start.9 = (bf16[512,512]{1,0:T(8,128)(2,1)S(1)}, bf16[512,512]{1,0:T(8,128)(2,1)}, u32[]{:S(2)}) copy-start(bf16[512,512]{1,0:T(8,128)(2,1)} %copy-done.8) | copy-start | bytes 1572868
  59.0 679.6 %reduce-scatter.2.cloned.1.call-start = ((), (), s32[]{:S(2)}) async-start(), calls=%async_computation.4 | async-start | bytes 5242880 | tf_op jit(solution)/shard_map/reduce_scatter | solution.py:92
  63.0 5.0 copy-start.13
  307.6 3.8 copy-start.4
  311.3 3.2 copy-start.1
  609.7 5.2 copy-start.5
  609.7 5.2 copy-start.7
  609.7 5.6 copy-start.10
  609.7 5.6 copy-start.14
  617.7 1.3 copy-start.3
  617.7 2.5 copy-start.11
  625.0 1.3 copy-start.2
Sparse Core Ops, SparseCore 0:
  9.1 33.3 all-gather.3
  50.9 256.6 all-gather.5
  309.4 300.2 all-gather.7
  638.8 99.7 reduce-scatter.1
where the time goes:
time: 747 us
  waiting for transfers between devices  667 us (89%)
  matrix products  43.8 us (6%)
  between operations  13.5 us (2%)
  local copies, waits for them, and re-layouts  12.2 us (2%)
  other arithmetic  10.5 us (1%)
    all_gather x1, waiting for transfers between devices, shards(): lax.all_gather(dilate(values_all), 'seq', axis=1, tiled=True)  294 us
    all_gather x1, waiting for transfers between devices, shards(): lax.all_gather(dilate(keys_all), 'seq', axis=1, tiled=True)  238 us
    reduce_scatter x1, waiting for transfers between devices, shards(): lax.psum_scatter(jnp.dot(context, w_out, preferred_element_type=jnp.float...  99.9 us
    all_gather x1, waiting for transfers between devices, shards(): piece = lax.all_gather(normed, 'sub', axis=0, tiled=True)  34.3 us
  transfers between devices with their start and end apart: 4, of which 4 were waited for; matrix products, arithmetic and copies ran while one was open for 3% of the time, Pallas kernels for 0%

commit v1 on v0

v1 whole, which is shorter than its diff:
```python
import functools
import math

import jax
import jax.numpy as jnp
from jax import lax
from jax.experimental import pallas as pl
from jax.experimental.pallas import tpu as pltpu
from jax.sharding import PartitionSpec as P

HEAD = 128
BLOCK = 128
KEPT = 16
MESH = pl.DeviceIdType.MESH
NX, NY, NZ = 2, 4, 8
SPANS = NX * NY * NZ
ROW_CUTS = 4
FIRST_CUTS = 2
LOG2E = 1.4426950408889634
NSLIDE = 8
HIDE = -1e30
ORDER = (0, 1, 3, 2)


def position():
    seq = lax.axis_index("seq")
    sub = lax.axis_index("sub")
    x = seq // (NY * NZ)
    y = (seq // NZ) % NY
    z = seq % NZ
    return seq, sub, x, y, z


def span_at(x, y, z):
    return x * (NY * NZ) + y * NZ + z


def remote(src, dst, send, recv, seq, sub):
    return pltpu.make_async_remote_copy(
        src_ref=src,
        dst_ref=dst,
        send_sem=send,
        recv_sem=recv,
        device_id=(seq, sub),
        device_id_type=MESH,
    )


def greet(places):
    barrier = pltpu.get_barrier_semaphore()
    for seq, sub in places:
        pl.semaphore_signal(barrier, inc=1, device_id=(seq, sub), device_id_type=MESH)
    pl.semaphore_wait(barrier, len(places))


class Ring:
    def __init__(self, turn, early, far, sems, place, counts):
        self.turn = turn
        self.early = early
        self.late = tuple(pair for pair in (0, 1) if pair not in early)
        self.far = far
        self.mate_recv, self.recv, self.send = sems
        self.place = place
        self.counts = counts
        self.sent = []
        self.flows = [(0, 0), (0, 1)] + [(1, pair) for pair in early]
        self.upward = set(self.flows[turn::2])

    def slot(self, r, other, pair):
        index = ((self.turn * NZ + r) * 2 + other) * 2 + pair
        return self.far.at[self.turn, r, other, 2 * pair : 2 * pair + 2], self.recv.at[index]

    def launch(self, src, dst, sem, place):
        index = self.counts[0]
        self.counts[0] = index + 1
        copy = remote(src, dst, self.send.at[index], sem, place, self.place[3])
        copy.start()
        self.sent.append(copy)

    def wait(self, r, other, pair):
        x, y, z, sub = self.place
        ref, sem = self.slot(r, other, pair)
        remote(ref, ref, self.send.at[0], sem, span_at(1 - x, y, z), sub).wait_recv()

    def put_x(self, r, pair):
        x, y, z, sub = self.place
        dst, sem = self.slot(r, 1, pair)
        self.launch(self.slot(r, 0, pair)[0], dst, sem, span_at(1 - x, y, z))

    def put_z(self, r, other, pair, step):
        x, y, z, sub = self.place
        dst, sem = self.slot((r - step) % NZ, other, pair)
        self.launch(self.slot(r, other, pair)[0], dst, sem, span_at(x, y, (z + step + NZ) % NZ))

    def begin(self, dil, own_sem):
        x, y, z, sub = self.place
        self.own = pltpu.make_async_copy(dil.at[y], self.far.at[self.turn, 0, 0, 0], own_sem)
        self.own.start()
        self.mates = []
        for dy in ORDER[1:]:
            head = (y + dy) % NY
            at = ORDER.index((NY - dy) % NY)
            dst = self.far.at[self.turn, 0, 0, at]
            self.launch(dil.at[head], dst, self.mate_recv.at[self.turn * NY + at], span_at(x, head, z))

    def wait_mate(self, at):
        x, y, z, sub = self.place
        dst = self.far.at[self.turn, 0, 0, at]
        remote(
            dst, dst, self.send.at[0], self.mate_recv.at[self.turn * NY + at],
            span_at(x, (y + 1) % NY, z), sub,
        ).wait_recv()

    def serve(self, d, others=(0, 1)):
        if d == 0:
            if 0 in others:
                self.own.wait()
                for pair in (0, 1):
                    for at in (2 * pair, 2 * pair + 1):
                        if at:
                            self.wait_mate(at)
                    self.put_x(0, pair)
                    self.put_z(0, 0, pair, 1)
                    self.put_z(0, 0, pair, -1)
            if 1 in others:
                for pair in self.early:
                    self.wait(0, 1, pair)
                    self.put_z(0, 1, pair, 1)
                    self.put_z(0, 1, pair, -1)
            return
        for flow in self.flows:
            other, pair = flow
            if other not in others:
                continue
            for up in (True, False):
                if d == 4 and up != (flow in self.upward):
                    continue
                r = NZ - d if up else d
                self.wait(r, other, pair)
                if d < 3 or (d == 3 and up == (flow in self.upward)):
                    self.put_z(r, other, pair, 1 if up else -1)
                if other == 0 and pair in self.late:
                    self.put_x(r, pair)

    def serve_late(self, d):
        for pair in self.late:
            for r in {0: (0,), 4: (4,)}.get(d, (NZ - d, d)):
                self.wait(r, 1, pair)


def exchange_kernel(
    len_ref, x_hbm, wq_hbm, wk_hbm, wv_hbm, wo_hbm, pat_ref, out_ref,
    xs, ws, qkv, pick, dil, far, group, keyed, turned, query, acc, peak,
    ctx_own, ctx, wo, away, home, give_mate, give_over, give_home, take_mate, take_over, take_home,
    local_sem, w_sem, own_sem, own_group_sem,
    mate_send, mate_recv, cross_send, cross_recv, pass_send, pass_recv,
    group_send, group_recv, near_recv, far_recv, ring_send,
    wo_sem, own_ctx_sem, ctx_send, ctx_recv,
    sum_send, sum_recv, over_send, over_recv, home_send, home_recv,
):
    seq, sub, x, y, z = position()
    core = sub % 2
    chip = sub // 2
    mate = sub + 1 - 2 * core
    over = (sub + 2) % 4
    rows = xs.shape[1]
    cut = rows // ROW_CUTS
    side_rows = 2 * rows
    span = 4 * rows
    blocks = span // BLOCK
    factor = LOG2E / math.sqrt(HEAD)

    own_x = pltpu.make_async_copy(x_hbm, xs.at[sub], local_sem)
    own_x.start()
    weights = []
    for index, (source, half) in enumerate(
        [(wk_hbm, 0), (wk_hbm, 1), (wv_hbm, 0), (wv_hbm, 1), (wq_hbm, 0), (wq_hbm, 1)]
    ):
        copy = pltpu.make_async_copy(
            source.at[:, half * 256 : (half + 1) * 256], ws.at[index], w_sem.at[index]
        )
        copy.start()
        weights.append(copy)

    load = pltpu.make_async_copy(wo_hbm, wo, wo_sem)
    load.start()
    side = span_at(1 - x, y, z)
    above = span_at(x, y, (z + 1) % NZ)
    below = span_at(x, y, (z + NZ - 1) % NZ)
    fellows = [span_at(x, (y + dy) % NY, z) for dy in (1, 2, 3)]
    greet(
        [(seq, mate), (seq, over), (side, sub), (above, sub), (below, sub)]
        + [(fellow, sub) for fellow in fellows]
    )

    to_mate = remote(x_hbm, xs.at[sub], mate_send, mate_recv, seq, mate)
    to_mate.start()
    crossing = []

    def cross(cuts):
        for r in cuts:
            part = slice(r * cut, (r + 1) * cut)
            copy = remote(
                x_hbm.at[part], xs.at[sub, part], cross_send.at[r], cross_recv.at[r], seq, over
            )
            copy.start()
            crossing.append(copy)

    cross(range(FIRST_CUTS))

    line = lax.broadcasted_iota(jnp.int32, (BLOCK, BLOCK), 0)
    for head in range(NY):
        hit = (line == pat_ref[head : head + 1, :]).astype(jnp.float32)
        pick[head] = hit.T[:KEPT, :].astype(jnp.bfloat16)

    def project(which, indices):
        lhs = xs[pl.ds(2 * which, 2)].reshape(side_rows, xs.shape[2])
        for index in indices:
            out = jnp.dot(lhs, ws[index], preferred_element_type=jnp.float32)
            if index > 3:
                out = out * factor
            out = out.astype(jnp.bfloat16)
            kind = (1, 2, 0)[index // 2]
            first = 2 * (index % 2)
            qkv[first, which, kind] = out[:, :HEAD]
            qkv[first + 1, which, kind] = out[:, HEAD:]

    half = 2 * KEPT

    def choose(which, into):
        for head in range(NY):
            for kind in (1, 2):
                for b in range(2):
                    taken = jnp.dot(
                        pick[head],
                        qkv[head, which, kind, b * BLOCK : (b + 1) * BLOCK, :],
                        preferred_element_type=jnp.float32,
                    )
                    base = (kind - 1) * half + b * KEPT
                    dil[into, head, base : base + KEPT, :] = taken.astype(jnp.bfloat16)

    counts = [0]
    sems = (near_recv, far_recv, ring_send)
    place = (x, y, z, sub)
    rings = [
        Ring(0, (0, 1), far, sems, place, counts),
        Ring(1, (0,), far, sems, place, counts),
    ]
    group_sent = []

    def share(which, turn):
        own = pltpu.make_async_copy(
            qkv.at[y, which], group.at[y, which], own_group_sem.at[turn]
        )
        own.start()
        for k, kinds in enumerate((slice(0, 1), slice(1, 3))):
            for dy in (1, 3, 2):
                head = (y + dy) % NY
                copy = remote(
                    qkv.at[head, which, kinds], group.at[y, which, kinds],
                    group_send.at[4 * dy + 2 * turn + k], group_recv.at[4 * y + 2 * which + k],
                    span_at(x, head, z), sub,
                )
                copy.start()
                group_sent.append(copy)
        return own

    def got_group(dy, k):
        fellow = (y + dy) % NY
        kinds = slice(1, 3) if k else slice(0, 1)
        for which in (chip, 1 - chip):
            remote(
                qkv.at[fellow, which, kinds], group.at[fellow, which, kinds],
                group_send.at[4], group_recv.at[4 * fellow + 2 * which + k],
                span_at(x, fellow, z), sub,
            ).wait_recv()

    own_x.wait()
    to_mate.wait_recv()
    for index in range(4):
        weights[index].wait()
    project(chip, range(4))
    choose(chip, 0)
    rings[0].begin(dil.at[0], own_sem.at[0])
    weights[4].wait()
    weights[5].wait()
    project(chip, (4, 5))
    own_groups = [share(chip, 0)]
    rings[0].serve(0, (0,))
    cross(range(FIRST_CUTS, ROW_CUTS))

    col = lax.broadcasted_iota(jnp.int32, (1, HEAD), 1)
    low = (col - NSLIDE) * blocks
    high = low + blocks
    total = jnp.int32(0)
    for j in range(NSLIDE):
        low = jnp.where(col == j, total, low)
        total = total + len_ref[j]
        high = jnp.where(col == j, total, high)
    flag = jnp.where(col < NSLIDE, 1.0, 0.0)
    line = lax.broadcasted_iota(jnp.int32, (span, HEAD), 0)

    def inside(block):
        return jnp.where((block >= low) & (block < high), 1.0, 0.0)

    pairs = [(turn, a, b) for turn in (0, 1) for a, b in ((7, 1), (6, 2), (5, 3), (0, 4))]
    turned[:, HEAD:, :] = jnp.ones((turned.shape[0], 16, span), jnp.bfloat16)

    def mark_chunk(c):
        turn, ra, rb = pairs[c]
        which = 1 - chip if turn else chip
        at = line % 128 // half
        at = jnp.where(at == 2, 3, jnp.where(at == 3, 2, at))
        away = jnp.where(line < 256, ra, rb)
        owner = span_at((x + line % 256 // 128) % NX, (y + at) % NY, (z + away) % NZ)
        block = owner * blocks + 2 * which + line % half // KEPT
        keyed[c, :, HEAD:] = (HIDE * jnp.abs(inside(block) - flag)).astype(jnp.bfloat16)

    def mark_span(item):
        mine = span_at(x, item, z)
        got = inside(mine * blocks + line // BLOCK)
        mark = flag * got + jnp.where(col == NSLIDE + mine, 1.0, 0.0)
        query[item, HEAD:, :] = mark.astype(jnp.bfloat16).T
        keyed[8 + item, :, HEAD:] = (HIDE * (flag * (1.0 - got))).astype(jnp.bfloat16)

    passing = []

    def hand_on(r):
        part = slice(r * cut, (r + 1) * cut)
        crossing[r].wait_recv()
        copy = remote(
            xs.at[over, part], xs.at[over, part], pass_send.at[r], pass_recv.at[r], seq, mate
        )
        copy.start()
        passing.append(copy)

    def marks(step):
        for c in (2 * step, 2 * step + 1):
            mark_chunk(c)
        mark_span(step)

    first, second = rings
    marks(0)
    first.serve(1, (0,))
    hand_on(0)
    marks(1)
    first.serve(2, (0,))
    hand_on(1)
    marks(2)
    first.serve(0, (1,))
    first.serve(3, (0,))
    hand_on(2)
    marks(3)
    acc[...] = jnp.zeros_like(acc)
    peak[...] = jnp.full_like(peak, 3 * HIDE)
    first.serve(1, (1,))
    first.serve(4, (0,))
    hand_on(3)
    for copy in passing:
        copy.wait_recv()
    project(1 - chip, range(4))
    choose(1 - chip, 1)
    second.begin(dil.at[1], own_sem.at[1])
    project(1 - chip, (4, 5))
    own_groups.append(share(1 - chip, 1))
    first.serve(2, (1,))

    def load_chunk(c):
        turn, ra, rb = pairs[c]
        for k, r in enumerate((ra, rb)):
            lines = slice(256 * k, 256 * (k + 1))
            keyed[c, lines, :HEAD] = far[turn, r, :, :, :half, :].reshape(256, HEAD)
            turned[c, :HEAD, lines] = far[turn, r, :, :, half:, :].reshape(256, HEAD).T

    def load_query(item):
        query[item, :HEAD, :] = group[item, :, 0].reshape(span, HEAD).T

    def load_near(item):
        keyed[8 + item, :, :HEAD] = group[item, :, 1].reshape(span, HEAD)
        turned[8 + item, :HEAD, :] = group[item, :, 2].reshape(span, HEAD).T

    def update(item, chunks):
        ask = query[item]
        found = [jnp.dot(keyed[c], ask, preferred_element_type=jnp.float32) for c in chunks]
        old = peak[item, :1, :]
        top = old
        for got in found:
            top = jnp.maximum(top, jnp.max(got, axis=0, keepdims=True))
        out = acc[item] * jnp.exp2(old - top)
        for c, got in zip(chunks, found):
            weight = jnp.exp2(got - top).astype(jnp.bfloat16)
            out = out + jnp.dot(turned[c], weight, preferred_element_type=jnp.float32)
        acc[item] = out
        peak[item] = jnp.broadcast_to(top, peak.shape[1:])

    def repeat(count, body):
        def step(k, carry):
            body(k)
            return carry

        lax.fori_loop(0, count, step, 0)

    for own in own_groups:
        own.wait()
    load_query(y)
    load_near(y)
    first.serve(3, (1,))
    second.serve(0, (0,))
    first.serve(4, (1,))
    second.serve(0, (1,))
    for c in range(4):
        load_chunk(c)
    repeat(2, lambda k: update(y, (2 * k, 2 * k + 1)))
    second.serve(1)
    second.serve_late(0)
    for dy in (1, 3):
        got_group(dy, 0)
        load_query((y + dy) % NY)
    repeat(2, lambda k: update((y + 1) % NY, (2 * k, 2 * k + 1)))
    second.serve(2)
    second.serve_late(1)
    repeat(2, lambda k: update((y + 3) % NY, (2 * k, 2 * k + 1)))
    got_group(2, 0)
    load_query((y + 2) % NY)
    second.serve(3)
    second.serve_late(2)
    load_chunk(4)
    load_chunk(5)
    repeat(2, lambda k: update((y + 2) % NY, (2 * k, 2 * k + 1)))
    second.serve(4)
    repeat(4, lambda k: update(k, (4, 5)))
    for dy in (1, 3, 2):
        got_group(dy, 1)
        load_near((y + dy) % NY)
    second.serve_late(3)
    load_chunk(6)
    repeat(4, lambda k: update(k, (6, 8 + k)))
    second.serve_late(4)
    load_chunk(7)

    def finish(item):
        update(item, (7,))
        out = acc[item, :HEAD, :] / acc[item, HEAD : HEAD + 1, :]
        ctx_own[item] = out.T.astype(jnp.bfloat16)

    pieces = away.shape[0]
    cols = away.shape[3]
    lane = pl.ds(pl.multiple_of(y * HEAD, HEAD), HEAD)
    sent = []
    incoming = [[], []]
    for dy in (1, 3, 2, 0):
        to = (y + dy) % NY
        finish(to)
        if dy == 0:
            own = pltpu.make_async_copy(ctx_own.at[y], ctx.at[:, lane], own_ctx_sem)
            own.start()
            continue
        for part in (0, 1):
            which = 1 - chip if part == 0 else chip
            lines = pl.ds(pl.multiple_of(which * 2 * rows, 2 * rows), 2 * rows)
            copy = remote(
                ctx_own.at[to, lines], ctx.at[lines, lane],
                ctx_send.at[2 * dy + part], ctx_recv.at[2 * dy + part], span_at(x, to, z), sub,
            )
            copy.start()
            sent.append(copy)
            incoming[part].append(copy)
    own.wait()
    load.wait()
    for copy in incoming[0]:
        copy.wait_recv()

    def product(which, piece):
        lines = pl.ds(pl.multiple_of(which * 2 * rows, 2 * rows), 2 * rows)
        return jnp.dot(
            ctx[lines, :], wo[:, piece * cols : (piece + 1) * cols],
            preferred_element_type=jnp.float32,
        ).reshape(2, rows, cols)

    to_partner = []
    to_over = []

    def forward(piece):
        to_partner[piece].wait_recv()
        total = away[piece, core] + take_mate[piece].astype(jnp.float32)
        give_over[piece] = total.astype(jnp.bfloat16)
        copy = remote(
            give_over.at[piece], take_over.at[piece],
            over_send.at[piece], over_recv.at[piece], seq, over,
        )
        copy.start()
        to_over.append(copy)

    for piece in range(pieces):
        away[piece] = product(1 - chip, piece)
        give_mate[piece] = away[piece, 1 - core].astype(jnp.bfloat16)
        copy = remote(
            give_mate.at[piece], take_mate.at[piece],
            sum_send.at[piece], sum_recv.at[piece], seq, mate,
        )
        copy.start()
        to_partner.append(copy)
        if piece:
            forward(piece - 1)
    forward(pieces - 1)

    for copy in incoming[1]:
        copy.wait_recv()
    to_home = []
    for piece in range(pieces):
        home[piece] = product(chip, piece)
        give_home[piece] = home[piece, 1 - core].astype(jnp.bfloat16)
        copy = remote(
            give_home.at[piece], take_home.at[piece],
            home_send.at[piece], home_recv.at[piece], seq, mate,
        )
        copy.start()
        to_home.append(copy)
    for piece in range(pieces):
        to_home[piece].wait_recv()
        to_over[piece].wait_recv()
        total = home[piece, core] + take_home[piece].astype(jnp.float32)
        total = total + take_over[piece].astype(jnp.float32)
        out_ref[:, piece * cols : (piece + 1) * cols] = total.astype(jnp.bfloat16)
    waiting = sent + to_partner + to_over + to_home
    for copy in waiting + [to_mate] + crossing + passing + group_sent + rings[0].sent + rings[1].sent:
        copy.wait_send()


def exchange(normed, w_query, w_key, w_value, w_out, pattern, slide_lengths):
    rows, width = normed.shape
    depth = w_out.shape[0]
    pieces = 4
    cols = width // pieces
    span = 4 * rows
    kept = 4 * KEPT
    any_spec = pl.BlockSpec(memory_space=pltpu.HBM)
    vmem_spec = pl.BlockSpec(memory_space=pltpu.VMEM)
    dma = pltpu.SemaphoreType.DMA
    vmem = pltpu.VMEM
    sums = vmem((pieces, 2, rows, cols), jnp.float32)
    parts = vmem((pieces, rows, cols), jnp.bfloat16)
    return pl.pallas_call(
        exchange_kernel,
        out_shape=jax.ShapeDtypeStruct((rows, width), jnp.bfloat16),
        in_specs=[pl.BlockSpec(memory_space=pltpu.SMEM)] + [any_spec] * 5 + [vmem_spec],
        out_specs=vmem_spec,
        scratch_shapes=[
            vmem((4, rows, width), jnp.bfloat16),
            vmem((6, width, 256), jnp.bfloat16),
            vmem((NY, 2, 3, span // 2, HEAD), jnp.bfloat16),
            vmem((NY, KEPT, BLOCK), jnp.bfloat16),
            vmem((2, NY, kept, HEAD), jnp.bfloat16),
            vmem((2, NZ, NX, NY, kept, HEAD), jnp.bfloat16),
            vmem((NY, 2, 3, span // 2, HEAD), jnp.bfloat16),
            vmem((8 + NY, span, 2 * HEAD), jnp.bfloat16),
            vmem((8 + NY, HEAD + 16, span), jnp.bfloat16),
            vmem((NY, 2 * HEAD, span), jnp.bfloat16),
            vmem((NY, HEAD + 16, span), jnp.float32),
            vmem((NY, 8, span), jnp.float32),
            vmem((NY, span, HEAD), jnp.bfloat16),
            vmem((span, depth), jnp.bfloat16),
            vmem((depth, width), jnp.bfloat16),
            sums, sums, parts, parts, parts, parts, parts, parts,
            dma, dma((6,)), dma((2,)), dma((2,)),
            dma, dma, dma((ROW_CUTS,)), dma((ROW_CUTS,)), dma((ROW_CUTS,)), dma((ROW_CUTS,)),
            dma((4 * NY,)), dma((4 * NY,)), dma((2 * NY,)), dma((4 * 2 * NZ,)), dma((80,)),
            dma, dma, dma((2 * NY,)), dma((2 * NY,)),
            dma((pieces,)), dma((pieces,)), dma((pieces,)), dma((pieces,)),
            dma((pieces,)), dma((pieces,)),
        ],
        compiler_params=pltpu.CompilerParams(
            collective_id=0, has_side_effects=True, vmem_limit_bytes=67043328
        ),
        name="exchange",
    )(slide_lengths, normed, w_query, w_key, w_value, w_out, pattern)


def shards(normed, w_query, w_key, w_value, w_out, pattern, slide_lengths):
    return exchange(normed, w_query, w_key, w_value, w_out, pattern, slide_lengths)


def solution(mesh):
    placed = (
        P(("seq", "sub"), None),
        P(None, "sub"),
        P(None, "sub"),
        P(None, "sub"),
        P("sub", None),
        P("sub", None),
        P(),
    )
    return jax.shard_map(
        shards, mesh=mesh, in_specs=placed, out_specs=P(("seq", "sub"), None), check_vma=False
    )
```

time: 747 us -> 90.5 us (0.12)
  waiting for transfers between devices: 667 us -> 0 us
  Pallas kernels: 0 us -> 88.4 us
  matrix products: 43.8 us -> 0 us
  between operations: 13.5 us -> 0.01 us
  other arithmetic: 10.5 us -> 0 us
  local copies, waits for them, and re-layouts: 12.2 us -> 1.88 us
    all_gather x3 -> x0, waiting for transfers between devices: 566 us -> none  [the longest x1 294 us: shards(): lax.all_gather(dilate(values_all), 'seq', axis=1, tiled=True)]
    reduce_scatter x1 -> x0, waiting for transfers between devices: 99.9 us -> none  [shards(): lax.psum_scatter(jnp.dot(context, w_out, preferred_element_type=jnp.float...]
    pallas_call x0 -> x1, Pallas kernels: none -> 88.4 us  [exchange(): pl.pallas_call(exchange_kernel, out_shape=jax.ShapeDtypeStruct((rows, wid...]
    dot_general x20 -> x0, matrix products: 43.8 us -> none  [the longest x4 11.4 us: shards(): jnp.dot(far_weight, far_values[head_index], preferred_element_type=jnp.fl...]
  transfers between devices with their start and end apart: 4 -> 0, of which waited for: 4 -> 0; matrix products, arithmetic and copies ran while one was open for 3% -> 0% of each run, Pallas kernels for 0% -> 0%
where the time goes in v1:
time: 90.5 us; the launch traced here: 90.3 us
  Pallas kernels  88.4 us (98%)
  local copies, waits for them, and re-layouts  1.88 us (2%)
    pallas_call x1, Pallas kernels, exchange(): pl.pallas_call(exchange_kernel, out_shape=jax.ShapeDtypeStruct((rows, wid...  88.4 us
    unnamed x1, local copies, waits for them, and re-layouts  1.88 us

profile of v1, /device:TPU:1, one launch (start us, length us, event | category | flops | bytes accessed | tf_op | source)
XLA Modules:
  0.0 90.3 jit_solution(4120203890945237539)
XLA Ops:
  0.0 88.4 %exchange.1 = bf16[128,2048]{1,0:T(8,128)(2,1)} custom-call(s32[8]{0:T(128)} %len_ref.1, bf16[128,2048]{1,0:T(8,128)(2,1)} %x_hbm.1, bf16[2048,512]{1,0:T(8,128)(2,1)} %wq_hbm.1, bf16[2048,512]{1,0:T(8,128)(2,1)} %wk_hbm.1, bf16[2048,512]{1,0:T(8,128)(2,1)} %wv_hbm.1, bf16[512,2048]{1,0:T(8,128)(2,1)} %wo_hbm.1, s32[4,128]{1,0:T(4,128)} %pat_ref.1), custom_call_target="tpu_custom_call" | custom-call | tf_op jit(solution)/shard_map/exchange/pallas_call | solution.py:543
  88.4 1.9 %copy.9 = bf16[128,2048]{1,0:T(8,128)(2,1)} copy(bf16[128,2048]{1,0:T(8,128)(2,1)} %exchange.1) | data formatting | bytes 1048576

commit v2 on v1

--- a/solution.py
+++ b/solution.py
@@ -354,7 +354,6 @@
     acc[...] = jnp.zeros_like(acc)
     peak[...] = jnp.full_like(peak, 3 * HIDE)
     first.serve(1, (1,))
-    first.serve(4, (0,))
     hand_on(3)
     for copy in passing:
         copy.wait_recv()
@@ -379,19 +378,30 @@
         keyed[8 + item, :, :HEAD] = group[item, :, 1].reshape(span, HEAD)
         turned[8 + item, :HEAD, :] = group[item, :, 2].reshape(span, HEAD).T
 
-    def update(item, chunks):
-        ask = query[item]
-        found = [jnp.dot(keyed[c], ask, preferred_element_type=jnp.float32) for c in chunks]
-        old = peak[item, :1, :]
-        top = old
-        for got in found:
-            top = jnp.maximum(top, jnp.max(got, axis=0, keepdims=True))
-        out = acc[item] * jnp.exp2(old - top)
-        for c, got in zip(chunks, found):
-            weight = jnp.exp2(got - top).astype(jnp.bfloat16)
-            out = out + jnp.dot(turned[c], weight, preferred_element_type=jnp.float32)
-        acc[item] = out
-        peak[item] = jnp.broadcast_to(top, peak.shape[1:])
+    def update(*tasks):
+        state = []
+        for item, chunks in tasks:
+            ask = query[item]
+            found = [jnp.dot(keyed[c], ask, preferred_element_type=jnp.float32) for c in chunks]
+            state.append((acc[item], peak[item, :1, :], found))
+        done = []
+        for (item, chunks), (total, old, found) in zip(tasks, state):
+            top = old
+            for got in found:
+                top = jnp.maximum(top, jnp.max(got, axis=0, keepdims=True))
+            out = total * jnp.exp2(old - top)
+            for c, got in zip(chunks, found):
+                weight = jnp.exp2(got - top).astype(jnp.bfloat16)
+                out = out + jnp.dot(turned[c], weight, preferred_element_type=jnp.float32)
+            done.append((out, top))
+        for (item, chunks), (out, top) in zip(tasks, done):
+            acc[item] = out
+            peak[item] = jnp.broadcast_to(top, peak.shape[1:])
+
+    def both(first_item, second_item, chunk_of):
+        return update(
+            (first_item, (chunk_of(first_item),)), (second_item, (chunk_of(second_item),))
+        )
 
     def repeat(count, body):
         def step(k, carry):
@@ -402,44 +412,51 @@
 
     for own in own_groups:
         own.wait()
+    after, before, across = (y + 1) % NY, (y + 3) % NY, (y + 2) % NY
     load_query(y)
     load_near(y)
+    load_chunk(0)
+    update((y, (8 + y, 0)))
+    second.serve(0, (0,))
     first.serve(3, (1,))
-    second.serve(0, (0,))
-    first.serve(4, (1,))
+    load_chunk(1)
+    load_chunk(2)
+    update((y, (1, 2)))
     second.serve(0, (1,))
-    for c in range(4):
-        load_chunk(c)
-    repeat(2, lambda k: update(y, (2 * k, 2 * k + 1)))
-    second.serve(1)
-    second.serve_late(0)
+    second.serve(1, (0,))
     for dy in (1, 3):
         got_group(dy, 0)
         load_query((y + dy) % NY)
-    repeat(2, lambda k: update((y + 1) % NY, (2 * k, 2 * k + 1)))
+    both(after, before, lambda item: 0)
+    second.serve(1, (1,))
+    second.serve_late(0)
+    first.serve(4)
+    load_chunk(3)
+    repeat(2, lambda k: both(after, before, lambda item: 1 + k))
     second.serve(2)
     second.serve_late(1)
-    repeat(2, lambda k: update((y + 3) % NY, (2 * k, 2 * k + 1)))
     got_group(2, 0)
-    load_query((y + 2) % NY)
+    load_query(across)
+    repeat(2, lambda k: update((across, (2 * k, 2 * k + 1))))
     second.serve(3)
     second.serve_late(2)
     load_chunk(4)
     load_chunk(5)
-    repeat(2, lambda k: update((y + 2) % NY, (2 * k, 2 * k + 1)))
+    both(after, before, lambda item: 3)
     second.serve(4)
-    repeat(4, lambda k: update(k, (4, 5)))
+    repeat(4, lambda k: both(k // 2 * 2, k // 2 * 2 + 1, lambda item: 4 + k % 2))
     for dy in (1, 3, 2):
         got_group(dy, 1)
         load_near((y + dy) % NY)
+    both(after, across, lambda item: 8 + item)
+    update((before, (8 + before,)), (y, (3,)))
     second.serve_late(3)
     load_chunk(6)
-    repeat(4, lambda k: update(k, (6, 8 + k)))
+    repeat(2, lambda k: both(2 * k, 2 * k + 1, lambda item: 6))
     second.serve_late(4)
     load_chunk(7)
 
     def finish(item):
-        update(item, (7,))
         out = acc[item, :HEAD, :] / acc[item, HEAD : HEAD + 1, :]
         ctx_own[item] = out.T.astype(jnp.bfloat16)
 
@@ -450,6 +467,8 @@
     incoming = [[], []]
     for dy in (1, 3, 2, 0):
         to = (y + dy) % NY
+        if dy in (1, 2):
+            both(to, (y + (3 if dy == 1 else 0)) % NY, lambda item: 7)
         finish(to)
         if dy == 0:
             own = pltpu.make_async_copy(ctx_own.at[y], ctx.at[:, lane], own_ctx_sem)

time: 90.5 us -> 84.1 us (0.929)
  Pallas kernels: 88.4 us -> 82 us
    pallas_call x1, Pallas kernels: 88.4 us -> 82 us  [exchange(): pl.pallas_call(exchange_kernel, out_shape=jax.ShapeDtypeStruct((rows, wid...]
where the time goes in v2:
time: 84.1 us; the launch traced here: 83.9 us
  Pallas kernels  82 us (98%)
  local copies, waits for them, and re-layouts  1.88 us (2%)
    pallas_call x1, Pallas kernels, exchange(): pl.pallas_call(exchange_kernel, out_shape=jax.ShapeDtypeStruct((rows, wid...  82 us
    unnamed x1, local copies, waits for them, and re-layouts  1.88 us

profile of v2, /device:TPU:1, one launch (start us, length us, event | category | flops | bytes accessed | tf_op | source)
XLA Modules:
  0.0 83.9 jit_solution(3624078850369805917)
XLA Ops:
  0.0 82.0 %exchange.1 = bf16[128,2048]{1,0:T(8,128)(2,1)} custom-call(s32[8]{0:T(128)} %len_ref.1, bf16[128,2048]{1,0:T(8,128)(2,1)} %x_hbm.1, bf16[2048,512]{1,0:T(8,128)(2,1)} %wq_hbm.1, bf16[2048,512]{1,0:T(8,128)(2,1)} %wk_hbm.1, bf16[2048,512]{1,0:T(8,128)(2,1)} %wv_hbm.1, bf16[512,2048]{1,0:T(8,128)(2,1)} %wo_hbm.1, s32[4,128]{1,0:T(4,128)} %pat_ref.1), custom_call_target="tpu_custom_call" | custom-call | tf_op jit(solution)/shard_map/exchange/pallas_call | solution.py:562
  82.0 1.9 %copy.9 = bf16[128,2048]{1,0:T(8,128)(2,1)} copy(bf16[128,2048]{1,0:T(8,128)(2,1)} %exchange.1) | data formatting | bytes 1048576
